TPU v7x, 32 devices: a whole 2x2x4 slice. The times are simulated.
32 devices in a mesh: replica: 4 (over x, core), fsdp: 8 (over z, y).
Axes of the slice: x: 2, y: 2, z: 4, core: 2. Of those that a mesh axis runs over, the one named last changes fastest.
Arguments:
- byte_input: bfloat16 [32768, 768], P(('replica', 'fsdp')), may hold values from -6 to 6
- global_out: bfloat16 [32768, 768], P(('replica', 'fsdp')), may hold values from -6 to 6
- cotangent: bfloat16 [32768, 768], P(('replica', 'fsdp')), may hold values from -6 to 6
- seq_patches: int32 [4, 4], P('replica'), may hold values from 1 to 512, 1024 in all within a row
- last_fill: int32 [4, 4], P('replica'), may hold values from 1 to 8
- deal_slots: int32 [4, 1024], P('replica', 'fsdp'), may hold values from 0 to 1023, as said below
- first_gain: bfloat16 [768], P('fsdp'), may hold values from 0.5 to 1.5
- first_shift: bfloat16 [768], P('fsdp'), may hold values from -1.796875 to 1.796875
- qkv_weight: bfloat16 [768, 2304], P('fsdp'), may hold values from -0.21875 to 0.21875
- out_weight: bfloat16 [768, 768], P('fsdp'), may hold values from -0.4375 to 0.4375
- second_gain: bfloat16 [768], P('fsdp'), may hold values from 0.5 to 1.5
- second_shift: bfloat16 [768], P('fsdp'), may hold values from -1.796875 to 1.796875
- up_weight: bfloat16 [768, 3072], P('fsdp'), may hold values from -0.21875 to 0.21875
- up_bias: bfloat16 [3072], P('fsdp'), may hold values from -3 to 3
- down_weight: bfloat16 [3072, 768], P('fsdp'), may hold values from -0.15625 to 0.15625
- down_bias: bfloat16 [768], P('fsdp'), may hold values from -1.796875 to 1.796875
Outputs:
- layer_out: bfloat16 [32768, 768], P(('replica', 'fsdp'))
- grad_input: bfloat16 [32768, 768], P(('replica', 'fsdp'))
- grad_global: bfloat16 [32768, 768], P(('replica', 'fsdp'))
- grad_first_gain: float32 [768], P('fsdp')
- grad_first_shift: float32 [768], P('fsdp')
- grad_qkv_weight: float32 [768, 2304], P('fsdp')
- grad_out_weight: float32 [768, 768], P('fsdp')
- grad_second_gain: float32 [768], P('fsdp')
- grad_second_shift: float32 [768], P('fsdp')
- grad_up_weight: float32 [768, 3072], P('fsdp')
- grad_up_bias: float32 [3072], P('fsdp')
- grad_down_weight: float32 [3072, 768], P('fsdp')
- grad_down_bias: float32 [768], P('fsdp')
Inputs may be any that keep to these rules, and one draw needn't show every extreme that they name: `seq_patches`: row g gives the patches of the 4 sequences of group g in order; each row sums to 1024 and its largest entry is 512. `last_fill`: bytes used in the last patch of each sequence; the rest of that patch is padding. Each row is a permutation of 0 to 1023. Of the patches p in any aligned block of 128, exactly 16 have deal_slots in each aligned block of 128 positions.
All inputs are finite; a program needn't handle non-finite values.
Results may differ from a plain program's by a relative error of at most 0.017.
Values may be sent and summed in bfloat16 or wider, within the bound.
No kernel may reach another device: no remote copies, remote signals or barrier semaphores. Data moves between devices by JAX's collectives and lax.ppermute only.
A program may use at most 128 MiB of HBM per device.

v0:
```python
import jax
import jax.numpy as jnp
from jax import lax
from jax.sharding import PartitionSpec as P

HEADS = 12
HEAD_DIM = 64
PATCH = 8
EPSILON = 1e-05


def contract_rows(left, right):
    return lax.dot_general(
        left, right, (((0,), (0,)), ((), ())), preferred_element_type=jnp.float32
    )


def contract_cols(left, right):
    return lax.dot_general(
        left, right, (((1,), (1,)), ((), ())), preferred_element_type=jnp.float32
    )


def apply_layer_normalize(values, gain, shift):
    center = values - jnp.mean(values, axis=1, keepdims=True)
    inverse = lax.rsqrt(jnp.mean(jnp.square(center), axis=1, keepdims=True) + EPSILON)
    normed = center * inverse
    return (normed * gain + shift, normed, inverse)


def normalize_pullback(upstream, gain, normed, inverse):
    scaled = upstream * gain
    inner = (
        scaled
        - jnp.mean(scaled, axis=1, keepdims=True)
        - normed * jnp.mean(scaled * normed, axis=1, keepdims=True)
    )
    return (inverse * inner, jnp.sum(upstream * normed, axis=0), jnp.sum(upstream, axis=0))


def block_mask(span):
    index = jnp.arange(span, dtype=jnp.int32)
    return (index[:, None] // PATCH == index[None, :] // PATCH) & (index[None, :] <= index[:, None])


def attention_scores(queries, keys_part, allowed):
    raw = jnp.einsum(
        "gqhd,gkhd->ghqk", queries, keys_part, preferred_element_type=jnp.float32
    ) * HEAD_DIM ** (-0.5)
    return jnp.where(allowed, raw, -1e30)


def body(
    byte_input,
    global_out,
    cotangent,
    seq_patches,
    last_fill,
    deal_slots,
    first_gain,
    first_shift,
    qkv_weight,
    out_weight,
    second_gain,
    second_shift,
    up_weight,
    up_bias,
    down_weight,
    down_bias,
):
    row_count = byte_input.shape[0]
    model_width = byte_input.shape[1]
    patch_count = row_count // PATCH
    fsdp_count = lax.axis_size("fsdp")
    share = patch_count // fsdp_count
    patch_ids = lax.axis_index("fsdp") * patch_count + jnp.arange(patch_count, dtype=jnp.int32)
    seq_ends = jnp.cumsum(seq_patches[0])
    seq_ids = jnp.sum((patch_ids[:, None] >= seq_ends[None, :]).astype(jnp.int32), axis=1)
    seq_hits = (seq_ids[:, None] == jnp.arange(seq_ends.shape[0], dtype=jnp.int32)[None, :]).astype(
        jnp.int32
    )
    end_of = jnp.sum(seq_hits * seq_ends[None, :], axis=1)
    fill_of = jnp.sum(seq_hits * last_fill[0][None, :], axis=1)
    in_patch = jnp.arange(PATCH, dtype=jnp.int32)
    keep_byte = (
        (patch_ids != end_of - 1)[:, None] | (in_patch[None, :] < fill_of[:, None])
    ).reshape(row_count, 1)
    target = deal_slots[0] // patch_count
    dealt_slot = deal_slots[0] % patch_count
    dest_hits = (target[:, None] == jnp.arange(fsdp_count, dtype=jnp.int32)[None, :]).astype(
        jnp.int32
    )
    dest_rank = jnp.sum((jnp.cumsum(dest_hits, axis=0) - 1) * dest_hits, axis=1)
    send_place = target * share + dest_rank
    send_order = (
        jnp.zeros((patch_count,), jnp.int32)
        .at[send_place]
        .set(jnp.arange(patch_count, dtype=jnp.int32))
    )

    def pack_rows(values):
        return values.reshape(patch_count, PATCH, model_width)[send_order].reshape(
            row_count, model_width
        )

    def unpack_rows(values):
        return values.reshape(patch_count, PATCH, model_width)[send_place].reshape(
            row_count, model_width
        )

    arrived, arrived_slot = (
        lax.all_to_all(pack_rows(byte_input), "fsdp", split_axis=0, concat_axis=0, tiled=True),
        lax.all_to_all(dealt_slot[send_order], "fsdp", split_axis=0, concat_axis=0, tiled=True),
    )
    (
        gain_full,
        complete_shift_vector,
        qkv_full,
        outproj_full,
        gain_later,
        deferred_shift_vector,
        expand_full,
        expand_bias,
        reduce_full,
        reduce_bias,
    ) = (
        lax.all_gather(first_gain, "fsdp", axis=0, tiled=True),
        lax.all_gather(first_shift, "fsdp", axis=0, tiled=True),
        lax.all_gather(qkv_weight, "fsdp", axis=0, tiled=True),
        lax.all_gather(out_weight, "fsdp", axis=0, tiled=True),
        lax.all_gather(second_gain, "fsdp", axis=0, tiled=True),
        lax.all_gather(second_shift, "fsdp", axis=0, tiled=True),
        lax.all_gather(up_weight, "fsdp", axis=0, tiled=True),
        lax.all_gather(up_bias, "fsdp", axis=0, tiled=True),
        lax.all_gather(down_weight, "fsdp", axis=0, tiled=True),
        lax.all_gather(down_bias, "fsdp", axis=0, tiled=True),
    )
    attention_norm_gain = gain_full.astype(jnp.float32)
    feedforward_norm_gain = gain_later.astype(jnp.float32)
    global_rows = global_out.reshape(patch_count, PATCH, model_width)[arrived_slot].reshape(
        row_count, model_width
    )
    residual_input = arrived.astype(jnp.float32) + global_rows.astype(jnp.float32)
    attention_normed_input, attention_centered_scaled, attention_inverse_deviation = (
        apply_layer_normalize(
            residual_input, attention_norm_gain, complete_shift_vector.astype(jnp.float32)
        )
    )
    first_in = attention_normed_input.astype(jnp.bfloat16)
    qkv_rows = jnp.dot(first_in, qkv_full, preferred_element_type=jnp.float32).astype(jnp.bfloat16)
    blocks = row_count // 128

    def heads_of(values, start):
        return lax.slice_in_dim(values, start, start + model_width, axis=1).reshape(
            blocks, 128, HEADS, HEAD_DIM
        )

    queries = heads_of(qkv_rows, 0)
    keys_part = heads_of(qkv_rows, model_width)
    values_part = heads_of(qkv_rows, 2 * model_width)
    allowed = block_mask(128)
    scores = attention_scores(queries, keys_part, allowed)
    top_score = jnp.max(scores, axis=3, keepdims=True)
    expo = jnp.exp(scores - top_score)
    total = jnp.sum(expo, axis=3, keepdims=True)
    log_total = top_score + jnp.log(total)
    probs = (expo / total).astype(jnp.bfloat16)
    mixed = jnp.einsum("ghqk,gkhd->gqhd", probs, values_part, preferred_element_type=jnp.float32)
    attended = mixed.reshape(row_count, model_width).astype(jnp.bfloat16)
    residual_midway = residual_input + jnp.dot(
        attended, outproj_full, preferred_element_type=jnp.float32
    )
    feedforward_normed_input, feedforward_centered_scaled, feedforward_inverse_deviation = (
        apply_layer_normalize(
            residual_midway, feedforward_norm_gain, deferred_shift_vector.astype(jnp.float32)
        )
    )
    second_in = feedforward_normed_input.astype(jnp.bfloat16)
    pre_act = jnp.dot(
        second_in, expand_full, preferred_element_type=jnp.float32
    ) + expand_bias.astype(jnp.float32)
    activ = jax.nn.gelu(pre_act, approximate=False).astype(jnp.bfloat16)
    result = (
        residual_midway
        + jnp.dot(activ, reduce_full, preferred_element_type=jnp.float32)
        + reduce_bias.astype(jnp.float32)
    )
    returned = lax.all_to_all(
        result.astype(jnp.bfloat16), "fsdp", split_axis=0, concat_axis=0, tiled=True
    )
    layer_out = jnp.where(keep_byte, unpack_rows(returned), jnp.zeros((), jnp.bfloat16))
    masked_cot = jnp.where(keep_byte, cotangent, jnp.zeros((), jnp.bfloat16))
    upstream_b = lax.all_to_all(
        pack_rows(masked_cot), "fsdp", split_axis=0, concat_axis=0, tiled=True
    )
    upstream = upstream_b.astype(jnp.float32)
    grad_reduce_bias = jnp.sum(upstream, axis=0)
    grad_reduce = contract_rows(activ, upstream_b)
    grad_activ = contract_cols(upstream_b, reduce_full)
    density = jnp.exp(-0.5 * jnp.square(pre_act)) * 0.3989422804014327
    cumulative = 0.5 * (1.0 + jax.scipy.special.erf(pre_act * 0.7071067811865476))
    grad_pre = (grad_activ * (cumulative + pre_act * density)).astype(jnp.bfloat16)
    grad_expand_bias = jnp.sum(grad_pre.astype(jnp.float32), axis=0)
    grad_expand = contract_rows(second_in, grad_pre)
    gradient_feedforward_branch = contract_cols(grad_pre, expand_full)
    normalize_piece, gradient_feedforward_gain, gradient_feedforward_shift = normalize_pullback(
        gradient_feedforward_branch,
        feedforward_norm_gain,
        feedforward_centered_scaled,
        feedforward_inverse_deviation,
    )
    grad_middle = upstream + normalize_piece
    grad_branch = grad_middle.astype(jnp.bfloat16)
    grad_outproj = contract_rows(attended, grad_branch)
    grad_attended = (
        contract_cols(grad_branch, outproj_full)
        .astype(jnp.bfloat16)
        .reshape(blocks, 128, HEADS, HEAD_DIM)
    )
    scores_again = attention_scores(queries, keys_part, allowed)
    probs_again = jnp.exp(scores_again - log_total)
    grad_probs = jnp.einsum(
        "gqhd,gkhd->ghqk", grad_attended, values_part, preferred_element_type=jnp.float32
    )
    grad_values = jnp.einsum(
        "ghqk,gqhd->gkhd",
        probs_again.astype(jnp.bfloat16),
        grad_attended,
        preferred_element_type=jnp.float32,
    )
    grad_scores = (
        probs_again * (grad_probs - jnp.sum(probs_again * grad_probs, axis=3, keepdims=True))
    ).astype(jnp.bfloat16)
    grad_queries = jnp.einsum(
        "ghqk,gkhd->gqhd", grad_scores, keys_part, preferred_element_type=jnp.float32
    ) * HEAD_DIM ** (-0.5)
    grad_keys = jnp.einsum(
        "ghqk,gqhd->gkhd", grad_scores, queries, preferred_element_type=jnp.float32
    ) * HEAD_DIM ** (-0.5)
    grad_qkv = jnp.concatenate(
        [
            grad_queries.reshape(row_count, model_width),
            grad_keys.reshape(row_count, model_width),
            grad_values.reshape(row_count, model_width),
        ],
        axis=1,
    ).astype(jnp.bfloat16)
    grad_qkv_full = contract_rows(first_in, grad_qkv)
    gradient_attention_branch = contract_cols(grad_qkv, qkv_full)
    normalize_before_attention, gradient_attention_gain, gradient_attention_shift = (
        normalize_pullback(
            gradient_attention_branch,
            attention_norm_gain,
            attention_centered_scaled,
            attention_inverse_deviation,
        )
    )
    grad_base = (grad_middle + normalize_before_attention).astype(jnp.bfloat16)
    inverse_slot = (
        jnp.zeros((patch_count,), jnp.int32)
        .at[arrived_slot]
        .set(jnp.arange(patch_count, dtype=jnp.int32))
    )
    grad_global = grad_base.reshape(patch_count, PATCH, model_width)[inverse_slot].reshape(
        row_count, model_width
    )
    sent_back = lax.all_to_all(grad_base, "fsdp", split_axis=0, concat_axis=0, tiled=True)
    grad_input = unpack_rows(sent_back)
    owned = (
        lax.psum_scatter(
            gradient_attention_gain.astype(jnp.bfloat16), "fsdp", scatter_dimension=0, tiled=True
        ).astype(jnp.float32),
        lax.psum_scatter(
            gradient_attention_shift.astype(jnp.bfloat16), "fsdp", scatter_dimension=0, tiled=True
        ).astype(jnp.float32),
        lax.psum_scatter(
            grad_qkv_full.astype(jnp.bfloat16), "fsdp", scatter_dimension=0, tiled=True
        ).astype(jnp.float32),
        lax.psum_scatter(
            grad_outproj.astype(jnp.bfloat16), "fsdp", scatter_dimension=0, tiled=True
        ).astype(jnp.float32),
        lax.psum_scatter(
            gradient_feedforward_gain.astype(jnp.bfloat16), "fsdp", scatter_dimension=0, tiled=True
        ).astype(jnp.float32),
        lax.psum_scatter(
            gradient_feedforward_shift.astype(jnp.bfloat16), "fsdp", scatter_dimension=0, tiled=True
        ).astype(jnp.float32),
        lax.psum_scatter(
            grad_expand.astype(jnp.bfloat16), "fsdp", scatter_dimension=0, tiled=True
        ).astype(jnp.float32),
        lax.psum_scatter(
            grad_expand_bias.astype(jnp.bfloat16), "fsdp", scatter_dimension=0, tiled=True
        ).astype(jnp.float32),
        lax.psum_scatter(
            grad_reduce.astype(jnp.bfloat16), "fsdp", scatter_dimension=0, tiled=True
        ).astype(jnp.float32),
        lax.psum_scatter(
            grad_reduce_bias.astype(jnp.bfloat16), "fsdp", scatter_dimension=0, tiled=True
        ).astype(jnp.float32),
    )
    totals = (
        lax.psum(owned[0].astype(jnp.bfloat16), "replica").astype(jnp.float32),
        lax.psum(owned[1].astype(jnp.bfloat16), "replica").astype(jnp.float32),
        lax.psum(owned[2].astype(jnp.bfloat16), "replica").astype(jnp.float32),
        lax.psum(owned[3].astype(jnp.bfloat16), "replica").astype(jnp.float32),
        lax.psum(owned[4].astype(jnp.bfloat16), "replica").astype(jnp.float32),
        lax.psum(owned[5].astype(jnp.bfloat16), "replica").astype(jnp.float32),
        lax.psum(owned[6].astype(jnp.bfloat16), "replica").astype(jnp.float32),
        lax.psum(owned[7].astype(jnp.bfloat16), "replica").astype(jnp.float32),
        lax.psum(owned[8].astype(jnp.bfloat16), "replica").astype(jnp.float32),
        lax.psum(owned[9].astype(jnp.bfloat16), "replica").astype(jnp.float32),
    )
    return (
        layer_out,
        grad_input,
        grad_global,
        totals[0],
        totals[1],
        totals[2],
        totals[3],
        totals[4],
        totals[5],
        totals[6],
        totals[7],
        totals[8],
        totals[9],
    )


def solution(mesh):
    in_specs = (
        P(("replica", "fsdp"), None),
        P(("replica", "fsdp"), None),
        P(("replica", "fsdp"), None),
        P("replica", None),
        P("replica", None),
        P("replica", "fsdp"),
        P("fsdp"),
        P("fsdp"),
        P("fsdp", None),
        P("fsdp", None),
        P("fsdp"),
        P("fsdp"),
        P("fsdp", None),
        P("fsdp"),
        P("fsdp", None),
        P("fsdp"),
    )
    out_specs = (
        P(("replica", "fsdp"), None),
        P(("replica", "fsdp"), None),
        P(("replica", "fsdp"), None),
        P("fsdp"),
        P("fsdp"),
        P("fsdp", None),
        P("fsdp", None),
        P("fsdp"),
        P("fsdp"),
        P("fsdp", None),
        P("fsdp"),
        P("fsdp", None),
        P("fsdp"),
    )
    return jax.shard_map(body, mesh=mesh, in_specs=in_specs, out_specs=out_specs, check_vma=False)
```

profile of v0, /device:TPU:0, one launch (start us, length us, event | category | flops | bytes accessed | tf_op | source)
XLA Modules:
  0.0 805.4 jit_solution(18170484477021151799)
XLA Ops:
  14.1 7.3 all-to-all-start.1
  23.3 4.5 all-to-all-done.1
  27.8 3.6 all-to-all-start
  34.2 50.6 %all-reduce.12 = (bf16[768]{0:T(1024)(128)(2,1)S(1)}, bf16[768]{0:T(1024)(128)(2,1)S(1)}, bf16[768]{0:T(1024)(128)(2,1)S(1)}, bf16[768]{0:T(1024)(128)(2,1)S(1)}) all-reduce(bf16[768]{0:T(1024)(128)(2,1)S(1)} %dynamic-update-slice.1, bf16[768]{0:T(1024)(128)(2,1)S(1)} %dynamic-update-slice, ...), channel_id=1, replica_groups=mesh['replica'=4,'fsdp'=8] {'fsdp'}, use_global_device_ids=true, to_apply=%add.1 | all-reduce | flops 3072 | bytes 12288
  84.8 43.5 %all-gather = bf16[8,1,384]{2,1,0:T(2,128)(2,1)S(1)} all-gather(bf16[1,1,384]{2,1,0:T(2,128)(2,1)S(1)} %reshape.552), channel_id=1, replica_groups=mesh['replica'=4,'fsdp'=8] {'fsdp'}, dimensions={0}, use_global_device_ids=true | all-gather | bytes 6912 | tf_op jit(solution)/shard_map/all_gather | solution.py:134
  133.9 2.1 gather_fusion.2
  135.9 2.1 convert_element_type.224
  138.0 4.3 all-to-all-start.3
  142.4 2.4 fusion.32
  146.5 3.0 add_convert_fusion.3
  149.5 6.3 convolution_convert_fusion
  157.2 2.8 copy.85
  160.1 3.0 copy.109
  164.7 3.1 copy.108
  177.7 3.9 fusion.60
  183.8 60.6 %all-gather.10.cloned.1.call-done = bf16[768,3072]{1,0:T(8,128)(2,1)} async-done(((bf16[96,3072]{1,0:T(8,128)(2,1)}), bf16[768,3072]{1,0:T(8,128)(2,1)}) %all-gather.10.cloned.1.call-update) | async-done | bytes 4718608 | tf_op jit(solution)/shard_map/all_gather | solution.py:133
  244.4 37.7 %fusion.2 = (bf16[1024,3072]{1,0:T(8,128)(2,1)}, f32[1024,3072]{1,0:T(8,128)}) fusion(f32[3072]{0:T(1024)S(1)} %bitcast.199, bf16[768,3072]{1,0:T(8,128)(2,1)} %all-gather.10.cloned.1.call-done, f32[1024,768]{1,0:T(8,128)} %copy-done.10, f32[768]{0:T(1024)S(1)} %convert_element_type.192, f32[768]{0:T(1024)S(1)} %convert_element_type.191, ...), kind=kOutput, calls=%fused_computation.12 | convolution fusion | flops 5043388416 | bytes 26765312 | tf_op jit(solution)/shard_map/dot_general | solution.py:179
  282.1 42.4 %all-gather.12.cloned.1.call-done = bf16[3072,768]{1,0:T(8,128)(2,1)} async-done(((bf16[384,768]{1,0:T(8,128)(2,1)}), bf16[3072,768]{1,0:T(8,128)(2,1)}) %all-gather.12.cloned.1.call-update) | async-done | bytes 4718608 | tf_op jit(solution)/shard_map/all_gather | solution.py:135
  324.5 12.5 %fusion.61 = (bf16[3072]{0:T(1024)(128)(2,1)S(1)}, bf16[1024,3072]{1,0:T(8,128)(2,1)S(1)}) fusion(f32[1024,3072]{1,0:T(8,128)} %get-tuple-element.60, f32[3072]{0:T(1024)S(1)} %bitcast.200, bf16[1024,768]{1,0:T(8,128)(2,1)} %bitcast.25, bf16[3072,768]{1,0:T(8,128)(2,1)} %all-gather.12.cloned.1.call-done), kind=kOutput, calls=%fused_computation.152 | convolution fusion | flops 4869583872 | bytes 25184256 | tf_op jit(solution)/shard_map/dot_general | solution.py:19
  337.1 5.7 multiply_reduce_fusion.1
  342.8 2.4 multiply_add_fusion
  346.9 2.4 fusion.23
  349.3 3.3 convolution_convert_fusion.4
  354.8 5.0 multiply_reduce_fusion
  359.8 2.0 multiply_convert_fusion.1
  363.4 3.5 fusion.27
  367.2 4.8 fusion.28
  374.5 5.0 fusion.29
  381.9 2.2 copy-done.20
  384.2 5.5 convolution_convert_fusion.3
  390.1 10.4 %convolution_convert_fusion.2 = bf16[768,3072]{1,0:T(8,128)(2,1)} fusion(bf16[1024,3072]{1,0:T(8,128)(2,1)} %copy-done.43, f32[1024,768]{1,0:T(8,128)} %copy-done.10, f32[768]{0:T(1024)S(1)} %convert_element_type.192, f32[768]{0:T(1024)S(1)} %convert_element_type.191, f32[1024]{0:T(1024)S(1)} %add_rsqrt_fusion, f32[1024]{0:T(1024)S(1)} %broadcast_multiply_fusion.4), kind=kOutput, calls=%fused_computation.38 | convolution fusion | flops 4838129664 | bytes 14170112 | tf_op jit(solution)/shard_map/dot_general | solution.py:13
  400.6 9.1 %convolution_convert_fusion.1 = bf16[3072,768]{1,0:T(8,128)(2,1)} fusion(bf16[1024,3072]{1,0:T(8,128)(2,1)} %get-tuple-element.59, bf16[1024,768]{1,0:T(8,128)(2,1)} %bitcast.25), kind=kOutput, calls=%fused_computation.37 | convolution fusion | flops 4834197504 | bytes 12582912 | tf_op jit(solution)/shard_map/dot_general | solution.py:13
  412.5 9.6 %multiply_reduce_fusion.2 = (bf16[768]{0:T(1024)(128)(2,1)S(1)}, f32[1024]{0:T(1024)S(1)}, f32[1024]{0:T(1024)S(1)}, bf16[768]{0:T(1024)(128)(2,1)S(1)}, f32[1024,768]{1,0:T(8,128)}) fusion(f32[1024]{0:T(1024)S(1)} %copy-done.26, f32[1024]{0:T(1024)S(1)} %copy-done.22, bf16[128,8,768]{2,1,0:T(8,128)(2,1)S(1)} %copy-done.8, ...), kind=kOutput, calls=%fused_computation.45 | convolution fusion | flops 3633312256 | bytes 14571520 | tf_op jit(solution)/shard_map/dot_general | solution.py:19
  422.1 35.5 %all-reduce.11 = (bf16[768]{0:T(1024)(128)(2,1)S(1)}, bf16[768]{0:T(1024)(128)(2,1)S(1)}, bf16[768]{0:T(1024)(128)(2,1)S(1)}, bf16[768]{0:T(1024)(128)(2,1)S(1)}...) all-reduce(bf16[768]{0:T(1024)(128)(2,1)S(1)} %dynamic-update-slice, ...), channel_id=1, replica_groups=mesh['replica'=4,'fsdp'=8] {'fsdp'}, use_global_device_ids=true, to_apply=%add.4 | all-reduce | flops 7680 | bytes 30720
  457.7 9.9 %add_convert_fusion.1 = bf16[1024,768]{1,0:T(8,128)(2,1)} fusion(f32[1024,768]{1,0:T(8,128)} %copy-done.10, bf16[1024,3072]{1,0:T(8,128)(2,1)} %get-tuple-element.59, bf16[3072,768]{1,0:T(8,128)(2,1)} %all-gather.12.cloned.1.call-done, f32[768]{0:T(1024)S(1)} %convert_element_type.196), kind=kOutput, calls=%fused_computation.53 | convolution fusion | flops 4834197504 | bytes 15731712 | tf_op jit(solution)/shard_map/dot_general | solution.py:185
  467.6 4.3 all-to-all-start.2
  471.9 4.4 add_convert_fusion
  476.4 28.1 %all-to-all-done.2 = bf16[8,128,768]{2,1,0:T(8,128)(2,1)} async-done(((bf16[8,128,768]{2,1,0:T(8,128)(2,1)}), bf16[8,128,768]{2,1,0:T(8,128)(2,1)}, u32[]{:S(2)}, u32[]{:S(2)}) %all-to-all-start.2) | async-done | bytes 1572896 | tf_op jit(solution)/shard_map/all_to_all | solution.py:188
  504.4 3.7 all-to-all-start.4
  508.2 30.2 %reduce-scatter.5.cloned.1.call-done = bf16[96,2304]{1,0:T(8,128)(2,1)} async-done(((bf16[768,2304]{1,0:T(8,128)(2,1)}), bf16[96,2304]{1,0:T(8,128)(2,1)}) %reduce-scatter.5.cloned.1.call-update) | async-done | bytes 442384 | tf_op jit(solution)/shard_map/reduce_scatter | solution.py:276
  538.4 105.4 %reduce-scatter.9.cloned.1.call-done = bf16[96,3072]{1,0:T(8,128)(2,1)} async-done(((bf16[768,3072]{1,0:T(8,128)(2,1)}), bf16[96,3072]{1,0:T(8,128)(2,1)}) %reduce-scatter.9.cloned.1.call-update) | async-done | bytes 589840 | tf_op jit(solution)/shard_map/reduce_scatter | solution.py:288
  643.8 98.9 %reduce-scatter.11.cloned.1.call-done = bf16[384,768]{1,0:T(8,128)(2,1)} async-done(((bf16[3072,768]{1,0:T(8,128)(2,1)}), bf16[384,768]{1,0:T(8,128)(2,1)}) %reduce-scatter.11.cloned.1.call-update) | async-done | bytes 589840 | tf_op jit(solution)/shard_map/reduce_scatter | solution.py:294
  745.6 6.8 all-reduce.13
  757.4 3.2 gather_fusion.3
  762.4 2.9 bitcast_select_fusion
  765.3 26.4 %all-reduce.17.cloned.1.call-done = (bf16[96,2304]{1,0:T(8,128)(2,1)}, bf16[96,768]{1,0:T(8,128)(2,1)}, bf16[96,3072]{1,0:T(8,128)(2,1)}, bf16[384,768]{1,0:T(8,128)(2,1)}) async-done(((bf16[96,2304]{1,0:T(8,128)(2,1)}, bf16[96,768]{1,0:T(8,128)(2,1)}, bf16[96,3072]{1,0:T(8,128)(2,1)}, bf16[384,768]{1,0:T(8,128)(2,1)}), (bf16[96,2304]{1,0:T(8,128)(2,1)}, bf16[96,768]{1,0:T(8,128)(2,1)}, ...) | async-done | bytes 1769488 | tf_op jit(solution)/shard_map/psum | solution.py:304
  791.7 2.0 convert_element_type.210
  795.4 2.2 convert_element_type.218
  (210 shorter events, 57.9 us)
Async XLA Ops:
  7.2 14.2 %copy-start = (bf16[1024,768]{1,0:T(8,128)(2,1)S(1)}, bf16[1024,768]{1,0:T(8,128)(2,1)}, u32[]{:S(2)}) copy-start(bf16[1024,768]{1,0:T(8,128)(2,1)} %param.16) | copy-start | bytes 4718596
  7.2 142.3 %all-gather.6.cloned.1.call-start = ((), (), s32[]{:S(2)}) async-start(), calls=%async_computation.9 | async-start | bytes 3981312 | tf_op jit(solution)/shard_map/all_gather | solution.py:129
  7.9 169.8 %all-gather.8.cloned.1.call-start = ((), (), s32[]{:S(2)}) async-start(), calls=%async_computation.10 | async-start | bytes 1327104 | tf_op jit(solution)/shard_map/all_gather | solution.py:130
  8.7 235.7 %all-gather.10.cloned.1.call-start = ((), (), s32[]{:S(2)}) async-start(), calls=%async_computation.11 | async-start | bytes 5308416 | tf_op jit(solution)/shard_map/all_gather | solution.py:133
  14.1 13.7 %all-to-all-start.1 = ((s32[8,16,1]{1,2,0:T(1,128)}), s32[8,16,1]{1,2,0:T(1,128)S(1)}, u32[]{:S(2)}, u32[]{:S(2)}) async-start(s32[8,16,1]{1,2,0:T(1,128)} %bitcast.11), calls=%async_computation.1 | async-start | bytes 8192 | tf_op jit(solution)/shard_map/all_to_all | solution.py:113
  21.4 10.6 %copy-start.29 = (u32[32]{0:T(128)S(1)}, u32[32]{0:T(128)}, u32[]{:S(2)}) copy-start(u32[32]{0:T(128)} %constant.168) | copy-start | bytes 388
  21.4 11.8 %copy-start.37 = (bf16[96]{0:T(256)(128)(2,1)S(1)}, bf16[96]{0:T(256)(128)(2,1)}, u32[]{:S(2)}) copy-start(bf16[96]{0:T(256)(128)(2,1)} %param.23) | copy-start | bytes 580
  21.4 12.1 %copy-start.38 = (bf16[96]{0:T(256)(128)(2,1)S(1)}, bf16[96]{0:T(256)(128)(2,1)}, u32[]{:S(2)}) copy-start(bf16[96]{0:T(256)(128)(2,1)} %param.22) | copy-start | bytes 580
  21.5 12.3 %copy-start.39 = (bf16[96]{0:T(256)(128)(2,1)S(1)}, bf16[96]{0:T(256)(128)(2,1)}, u32[]{:S(2)}) copy-start(bf16[96]{0:T(256)(128)(2,1)} %param.27) | copy-start | bytes 580
  21.5 12.5 %copy-start.40 = (bf16[96]{0:T(256)(128)(2,1)S(1)}, bf16[96]{0:T(256)(128)(2,1)}, u32[]{:S(2)}) copy-start(bf16[96]{0:T(256)(128)(2,1)} %param.26) | copy-start | bytes 580
  21.5 63.3 %copy-start.30 = (bf16[384]{0:T(512)(128)(2,1)S(1)}, bf16[384]{0:T(512)(128)(2,1)}, u32[]{:S(2)}) copy-start(bf16[384]{0:T(512)(128)(2,1)} %param.29) | copy-start | bytes 2308
  21.5 106.8 %copy-start.41 = (s32[1,4]{1,0:T(1,128)S(1)}, s32[1,4]{1,0:T(1,128)}, u32[]{:S(2)}) copy-start(s32[1,4]{1,0:T(1,128)} %param.19) | copy-start | bytes 52
  21.5 107.1 %copy-start.31 = (s32[1,4]{1,0:T(1,128)S(1)}, s32[1,4]{1,0:T(1,128)}, u32[]{:S(2)}) copy-start(s32[1,4]{1,0:T(1,128)} %param.20) | copy-start | bytes 52
  27.8 110.2 %all-to-all-start = ((bf16[8,128,768]{2,1,0:T(8,128)(2,1)}), bf16[8,128,768]{2,1,0:T(8,128)(2,1)S(1)}, u32[]{:S(2)}, u32[]{:S(2)}) async-start(bf16[8,128,768]{2,1,0:T(8,128)(2,1)} %bitcast.8), calls=%async_computation | async-start | bytes 3145728 | tf_op jit(solution)/shard_map/all_to_all | solution.py:112
  31.4 293.1 %all-gather.12.cloned.1.call-start = ((), (), s32[]{:S(2)}) async-start(), calls=%async_computation.12 | async-start | bytes 5308416 | tf_op jit(solution)/shard_map/all_gather | solution.py:135
  84.8 61.1 %copy-start.23 = (f32[768]{0:T(1024)}, f32[768]{0:T(1024)S(1)}, u32[]{:S(2)}) copy-start(f32[768]{0:T(1024)S(1)} %convert_element_type.183) | copy-start | bytes 9220
  128.9 3.6 copy-start.27
  133.8 4.2 copy-start.34
  135.9 10.0 %copy-start.7 = (bf16[128,8,768]{2,1,0:T(8,128)(2,1)}, bf16[128,8,768]{2,1,0:T(8,128)(2,1)S(1)}, u32[]{:S(2)}) copy-start(bf16[128,8,768]{2,1,0:T(8,128)(2,1)S(1)} %gather_fusion.2) | copy-start | bytes 4718596
  138.0 7.9 copy-start.3
  138.0 144.1 %all-to-all-start.3 = ((bf16[8,128,768]{2,1,0:T(8,128)(2,1)}), bf16[8,128,768]{2,1,0:T(8,128)(2,1)}, u32[]{:S(2)}, u32[]{:S(2)}) async-start(bf16[8,128,768]{2,1,0:T(8,128)(2,1)} %bitcast.186), calls=%async_computation.3 | async-start | bytes 3145728 | tf_op jit(solution)/shard_map/all_to_all | solution.py:193
  142.3 365.8 %reduce-scatter.7.cloned.1.call-start = ((), (), s32[]{:S(2)}) async-start(), calls=%async_computation.14 | async-start | bytes 1327104 | tf_op jit(solution)/shard_map/reduce_scatter | solution.py:279
  142.4 2.8 copy-start.5
  169.1 5.1 copy-start.16
  172.6 2.6 copy-start.2
  324.5 12.5 %copy-start.11 = (f32[1024,768]{1,0:T(8,128)S(1)}, f32[1024,768]{1,0:T(8,128)}, u32[]{:S(2)}) copy-start(f32[1024,768]{1,0:T(8,128)} %copy-done.10) | copy-start | bytes 9437188
  324.5 12.6 %copy-start.35 = (bf16[768,3072]{1,0:T(8,128)(2,1)S(1)}, bf16[768,3072]{1,0:T(8,128)(2,1)}, u32[]{:S(2)}) copy-start(bf16[768,3072]{1,0:T(8,128)(2,1)} %all-gather.10.cloned.1.call-done) | copy-start | bytes 14155780
  337.0 5.7 copy-start.43
  353.8 5.9 slice-start
  354.8 5.0 slice-start.1
  367.0 5.0 copy-start.15
  367.0 171.4 %reduce-scatter.5.cloned.1.call-start = ((), (), s32[]{:S(2)}) async-start(), calls=%async_computation.13 | async-start | bytes 3981312 | tf_op jit(solution)/shard_map/reduce_scatter | solution.py:276
  381.1 3.0 copy-start.18
  389.7 254.1 %reduce-scatter.9.cloned.1.call-start = ((), (), s32[]{:S(2)}) async-start(), calls=%async_computation.15 | async-start | bytes 5308416 | tf_op jit(solution)/shard_map/reduce_scatter | solution.py:288
  400.6 342.1 %reduce-scatter.11.cloned.1.call-start = ((), (), s32[]{:S(2)}) async-start(), calls=%async_computation.16 | async-start | bytes 5308416 | tf_op jit(solution)/shard_map/reduce_scatter | solution.py:294
  409.7 2.7 copy-start.4
  409.7 2.7 copy-start.8
  409.8 2.7 copy-start.22
  409.8 2.7 copy-start.24
  409.8 2.7 copy-start.26
  467.6 36.8 %all-to-all-start.2 = ((bf16[8,128,768]{2,1,0:T(8,128)(2,1)}), bf16[8,128,768]{2,1,0:T(8,128)(2,1)}, u32[]{:S(2)}, u32[]{:S(2)}) async-start(bf16[8,128,768]{2,1,0:T(8,128)(2,1)} %bitcast.195), calls=%async_computation.2 | async-start | bytes 3145728 | tf_op jit(solution)/shard_map/all_to_all | solution.py:188
  476.3 267.6 %copy-start.33 = (s32[128]{0:T(128)S(1)}, s32[128]{0:T(128)}, u32[]{:S(2)}) copy-start(s32[128]{0:T(128)} %copy-done.32) | copy-start | bytes 1540
  476.3 279.2 %copy-start.9 = (bf16[1024,768]{1,0:T(8,128)(2,1)S(1)}, bf16[1024,768]{1,0:T(8,128)(2,1)}, u32[]{:S(2)}) copy-start(bf16[1024,768]{1,0:T(8,128)(2,1)} %add_convert_fusion) | copy-start | bytes 4718596
  504.4 256.2 %all-to-all-start.4 = ((bf16[8,128,768]{2,1,0:T(8,128)(2,1)}), bf16[8,128,768]{2,1,0:T(8,128)(2,1)S(1)}, u32[]{:S(2)}, u32[]{:S(2)}) async-start(bf16[8,128,768]{2,1,0:T(8,128)(2,1)} %bitcast.174), calls=%async_computation.4 | async-start | bytes 3145728 | tf_op jit(solution)/shard_map/all_to_all | solution.py:267
  508.1 283.6 %all-reduce.17.cloned.1.call-start = ((), (), s32[]{:S(2)}) async-start(), calls=%async_computation.17 | async-start | bytes 3538944 | tf_op jit(solution)/shard_map/psum | solution.py:304
  757.4 5.0 copy-start.28
  762.4 36.2 %copy-start.1 = (bf16[1024,768]{1,0:T(8,128)(2,1)S(1)}, bf16[1024,768]{1,0:T(8,128)(2,1)}, u32[]{:S(2)}) copy-start(bf16[1024,768]{1,0:T(8,128)(2,1)} %param.16) | copy-start | bytes 4718596
  791.7 5.9 copy-start.19
  (12 other events, 18.3 us)
Sparse Core Ops, SparseCore 0:
  10.2 92.3 all-gather.5
  104.8 45.2 all-gather.7
  152.3 92.0 all-gather.9
  246.4 78.0 all-gather.11
  367.1 62.1 reduce-scatter.6
  432.8 105.5 reduce-scatter.4
  542.0 101.7 reduce-scatter.8
  647.4 95.2 reduce-scatter.10
  745.3 46.3 all-reduce.16
where the time goes:
time: 813 us; the launch traced here: 805 us
  waiting for transfers between devices  399 us (49%)
  matrix products  137 us (17%)
  blocking collectives  136 us (17%)
  local copies, waits for them, and re-layouts  52.6 us (6%)
  other arithmetic  38.7 us (5%)
  starting transfers between devices  24.1 us (3%)
  between operations  16.9 us (2%)
    reduce_scatter x1, waiting for transfers between devices, body(): lax.psum_scatter(grad_expand.astype(jnp.bfloat16), 'fsdp', scatter_dimens...  105 us
    reduce_scatter x1, waiting for transfers between devices, body(): lax.psum_scatter(grad_reduce.astype(jnp.bfloat16), 'fsdp', scatter_dimens...  98.9 us
    unnamed x2, blocking collectives  86.1 us
    all_gather x1, waiting for transfers between devices, body(): lax.all_gather(up_weight, 'fsdp', axis=0, tiled=True)  60.6 us
    all_gather x1, blocking collectives, body(): lax.all_gather(up_bias, 'fsdp', axis=0, tiled=True)  43.5 us
    all_gather x1, waiting for transfers between devices, body(): lax.all_gather(down_weight, 'fsdp', axis=0, tiled=True)  42.4 us
    dot_general x1, matrix products, body(): jnp.dot(second_in, expand_full, preferred_element_type=jnp.float32)  37.7 us
    dot_general x4, matrix products, contract_cols(): lax.dot_general(left, right, (((1,), (1,)), ((), ())), preferred_element_...  31.2 us
  transfers between devices with their start and end apart: 14, of which 8 were waited for; matrix products, arithmetic and copies ran while one was open for 21% of the time, Pallas kernels for 0%

commit v1 on v0

--- a/solution.py
+++ b/solution.py
@@ -7,6 +7,19 @@
 HEAD_DIM = 64
 PATCH = 8
 EPSILON = 1e-05
+
+
+def ring_gather(x, axis, dim):
+    ways = lax.axis_size(axis)
+    up = [(d, (d + 1) % ways) for d in range(ways)]
+    down = [(d, (d - 1) % ways) for d in range(ways)]
+    earlier, later = ([x], [x])
+    for _ in range(ways // 2):
+        earlier.append(lax.ppermute(earlier[-1], axis, up))
+    for _ in range((ways - 1) // 2):
+        later.append(lax.ppermute(later[-1], axis, down))
+    line = jnp.concatenate([*earlier[::-1], *later[1:]], axis=dim)
+    return jnp.roll(line, (lax.axis_index(axis) - ways // 2) * x.shape[dim], axis=dim)
 
 
 def contract_rows(left, right):
@@ -132,7 +145,7 @@
         lax.all_gather(second_shift, "fsdp", axis=0, tiled=True),
         lax.all_gather(up_weight, "fsdp", axis=0, tiled=True),
         lax.all_gather(up_bias, "fsdp", axis=0, tiled=True),
-        lax.all_gather(down_weight, "fsdp", axis=0, tiled=True),
+        ring_gather(down_weight, "fsdp", 0),
         lax.all_gather(down_bias, "fsdp", axis=0, tiled=True),
     )
     attention_norm_gain = gain_full.astype(jnp.float32)

time: 813 us -> 826 us (1.016)
  waiting for transfers between devices: 399 us -> 354 us
  starting transfers between devices: 24.1 us -> 46.9 us
  local copies, waits for them, and re-layouts: 52.6 us -> 73.9 us
  blocking collectives: 136 us -> 150 us
    ppermute x0 -> x7, waiting for transfers between devices: none -> 66.1 us  [the longest x4 65 us: ring_gather(): earlier.append(lax.ppermute(earlier[-1], axis, up))]
    all_gather x1 -> x0, waiting for transfers between devices: 42.4 us -> none  [body(): lax.all_gather(down_weight, 'fsdp', axis=0, tiled=True)]
    all_gather x1, waiting for transfers between devices: 60.6 us -> 26.9 us  [body(): lax.all_gather(up_weight, 'fsdp', axis=0, tiled=True)]
    unnamed x2, blocking collectives: 86.1 us -> 115 us
    all_to_all x1, waiting for transfers between devices: 28.1 us -> 0.01 us  [body(): lax.all_to_all(result.astype(jnp.bfloat16), 'fsdp', split_axis=0, concat_...]
    unnamed x116 -> x131, local copies, waits for them, and re-layouts: 22.7 us -> 44.1 us
    ppermute x0 -> x7, starting transfers between devices: none -> 19.3 us  [the longest x3 11.1 us: ring_gather(): later.append(lax.ppermute(later[-1], axis, down))]
    all_gather x1, blocking collectives: 43.5 us -> 28.1 us  [body(): lax.all_gather(up_bias, 'fsdp', axis=0, tiled=True)]
  transfers between devices with their start and end apart: 14 -> 20, of which waited for: 8 -> 9; matrix products, arithmetic and copies ran while one was open for 21% -> 23% of each run, Pallas kernels for 0% -> 0%
where the time goes in v1:
time: 826 us; the launch traced here: 817 us
  waiting for transfers between devices  354 us (43%)
  blocking collectives  150 us (18%)
  matrix products  134 us (16%)
  local copies, waits for them, and re-layouts  73.9 us (9%)
  starting transfers between devices  46.9 us (6%)
  other arithmetic  40.6 us (5%)
  between operations  17.2 us (2%)
    unnamed x2, blocking collectives  115 us
    reduce_scatter x1, waiting for transfers between devices, body(): lax.psum_scatter(grad_expand.astype(jnp.bfloat16), 'fsdp', scatter_dimens...  102 us
    reduce_scatter x1, waiting for transfers between devices, body(): lax.psum_scatter(grad_reduce.astype(jnp.bfloat16), 'fsdp', scatter_dimens...  98.8 us
    ppermute x4, waiting for transfers between devices, ring_gather(): earlier.append(lax.ppermute(earlier[-1], axis, up))  65 us
    unnamed x131, local copies, waits for them, and re-layouts  44.1 us
    dot_general x1, matrix products, body(): jnp.dot(second_in, expand_full, preferred_element_type=jnp.float32)  37.3 us
    dot_general x4, matrix products, contract_cols(): lax.dot_general(left, right, (((1,), (1,)), ((), ())), preferred_element_...  30.3 us
    psum x1, waiting for transfers between devices, body(): lax.psum(owned[2].astype(jnp.bfloat16), 'replica').astype(jnp.float32)  29.4 us
  transfers between devices with their start and end apart: 20, of which 9 were waited for; matrix products, arithmetic and copies ran while one was open for 23% of the time, Pallas kernels for 0%

profile of v1, /device:TPU:0, one launch (start us, length us, event | category | flops | bytes accessed | tf_op | source)
XLA Modules:
  0.0 816.8 jit_solution(1610542844917491267)
XLA Ops:
  8.7 3.0 collective-permute-start
  11.7 3.1 collective-permute-start.4
  17.6 24.4 %collective-permute-done = bf16[384,768]{1,0:T(8,128)(2,1)S(1)} collective-permute-done((bf16[384,768]{1,0:T(8,128)(2,1)}, bf16[384,768]{1,0:T(8,128)(2,1)S(1)}, u32[]{:S(2)}, u32[]{:S(2)}) %collective-permute-start) | collective-permute-done | bytes 589856 | tf_op jit(solution)/shard_map/ppermute | solution.py:18
  42.0 2.4 collective-permute-start.1
  46.3 4.9 all-to-all-start.1
  53.6 11.9 %collective-permute-done.1 = bf16[384,768]{1,0:T(8,128)(2,1)} collective-permute-done((bf16[384,768]{1,0:T(8,128)(2,1)S(1)}, bf16[384,768]{1,0:T(8,128)(2,1)}, u32[]{:S(2)}, u32[]{:S(2)}) %collective-permute-start.1) | collective-permute-done | bytes 589856 | tf_op jit(solution)/shard_map/ppermute | solution.py:18
  67.6 6.1 all-to-all-start
  75.4 4.8 collective-permute-start.5
  80.1 28.7 %collective-permute-done.2 = bf16[384,768]{1,0:T(8,128)(2,1)} collective-permute-done((bf16[384,768]{1,0:T(8,128)(2,1)}, bf16[384,768]{1,0:T(8,128)(2,1)}, u32[]{:S(2)}, u32[]{:S(2)}) %collective-permute-start.2) | collective-permute-done | bytes 589856 | tf_op jit(solution)/shard_map/ppermute | solution.py:18
  108.8 2.8 collective-permute-start.3
  113.8 37.6 %all-reduce.12 = (bf16[768]{0:T(1024)(128)(2,1)S(1)}, bf16[768]{0:T(1024)(128)(2,1)S(1)}, bf16[768]{0:T(1024)(128)(2,1)S(1)}, bf16[768]{0:T(1024)(128)(2,1)S(1)}) all-reduce(bf16[768]{0:T(1024)(128)(2,1)S(1)} %dynamic-update-slice.1, bf16[768]{0:T(1024)(128)(2,1)S(1)} %dynamic-update-slice, ...), channel_id=1, replica_groups=mesh['replica'=4,'fsdp'=8] {'fsdp'}, use_global_device_ids=true, to_apply=%add.1 | all-reduce | flops 3072 | bytes 12288
  151.6 28.1 %all-gather = bf16[8,1,384]{2,1,0:T(2,128)(2,1)S(1)} all-gather(bf16[1,1,384]{2,1,0:T(2,128)(2,1)S(1)} %reshape.552), channel_id=1, replica_groups=mesh['replica'=4,'fsdp'=8] {'fsdp'}, dimensions={0}, use_global_device_ids=true | all-gather | bytes 6912 | tf_op jit(solution)/shard_map/all_gather | solution.py:147
  186.9 3.2 collective-permute-start.6
  215.8 6.4 all-to-all-start.3
  222.3 2.4 fusion.37
  226.4 3.0 add_convert_fusion.3
  229.4 6.3 convolution_convert_fusion
  237.1 3.0 copy.83
  240.1 3.1 copy.107
  244.8 3.0 copy.109
  256.7 3.9 fusion.67
  262.9 26.9 %all-gather.9.cloned.1.call-done = bf16[768,3072]{1,0:T(8,128)(2,1)} async-done(((bf16[96,3072]{1,0:T(8,128)(2,1)}), bf16[768,3072]{1,0:T(8,128)(2,1)}) %all-gather.9.cloned.1.call-update) | async-done | bytes 4718608 | tf_op jit(solution)/shard_map/all_gather | solution.py:146
  289.8 37.3 %fusion.2 = (bf16[1024,3072]{1,0:T(8,128)(2,1)}, f32[1024,3072]{1,0:T(8,128)}) fusion(f32[3072]{0:T(1024)S(1)} %bitcast.197, bf16[768,3072]{1,0:T(8,128)(2,1)} %all-gather.9.cloned.1.call-done, f32[1024,768]{1,0:T(8,128)} %copy-done.9, f32[768]{0:T(1024)S(1)} %convert_element_type.192, f32[768]{0:T(1024)S(1)} %convert_element_type.191, ...), kind=kOutput, calls=%fused_computation.12 | convolution fusion | flops 5043388416 | bytes 26765312 | tf_op jit(solution)/shard_map/dot_general | solution.py:192
  327.1 13.0 %fusion.68 = (bf16[3072]{0:T(1024)(128)(2,1)S(1)}, bf16[1024,3072]{1,0:T(8,128)(2,1)S(1)}) fusion(f32[1024,3072]{1,0:T(8,128)} %get-tuple-element.60, f32[3072]{0:T(1024)S(1)} %bitcast.198, bf16[1024,768]{1,0:T(8,128)(2,1)} %bitcast.25, bf16[6144,768]{1,0:T(8,128)(2,1)} %constant_dynamic-update-slice_fusion, s32[]{:T(128)S(6)} %select_n.106), kind=kOutput, calls=%fused_computation.173 | convolution fusion | flops 4869583872 | bytes 25184260 | tf_op jit(solution)/shard_map/dot_general | solution.py:32
  340.1 5.7 multiply_reduce_fusion.1
  345.8 2.4 multiply_add_fusion
  349.9 2.4 fusion.28
  352.3 3.3 convolution_convert_fusion.4
  356.8 5.2 fusion.34
  362.0 7.2 multiply_reduce_fusion
  370.9 6.5 multiply_convert_fusion.1
  379.8 2.3 fusion.33
  384.5 2.1 copy-done.24
  386.6 5.5 convolution_convert_fusion.3
  392.3 10.5 %convolution_convert_fusion.2 = bf16[768,3072]{1,0:T(8,128)(2,1)} fusion(bf16[1024,3072]{1,0:T(8,128)(2,1)} %copy-done.45, f32[1024,768]{1,0:T(8,128)} %copy-done.9, f32[768]{0:T(1024)S(1)} %convert_element_type.192, f32[768]{0:T(1024)S(1)} %convert_element_type.191, f32[1024]{0:T(1024)S(1)} %add_rsqrt_fusion, f32[1024]{0:T(1024)S(1)} %broadcast_multiply_fusion.4), kind=kOutput, calls=%fused_computation.38 | convolution fusion | flops 4838129664 | bytes 14170112 | tf_op jit(solution)/shard_map/dot_general | solution.py:26
  402.9 9.2 %convolution_convert_fusion.1 = bf16[3072,768]{1,0:T(8,128)(2,1)} fusion(bf16[1024,3072]{1,0:T(8,128)(2,1)} %get-tuple-element.59, bf16[1024,768]{1,0:T(8,128)(2,1)} %bitcast.25), kind=kOutput, calls=%fused_computation.37 | convolution fusion | flops 4834197504 | bytes 12582912 | tf_op jit(solution)/shard_map/dot_general | solution.py:26
  414.0 8.3 %multiply_reduce_fusion.2 = (bf16[768]{0:T(1024)(128)(2,1)S(1)}, f32[1024]{0:T(1024)S(1)}, f32[1024]{0:T(1024)S(1)}, bf16[768]{0:T(1024)(128)(2,1)S(1)}, f32[1024,768]{1,0:T(8,128)S(1)}) fusion(f32[1024]{0:T(1024)S(1)} %copy-done.30, f32[1024]{0:T(1024)S(1)} %copy-done.26, bf16[128,8,768]{2,1,0:T(8,128)(2,1)S(1)} %copy-done.7, ...), kind=kOutput, calls=%fused_computation.48 | convolution fusion | flops 3633312256 | bytes 14571520 | tf_op jit(solution)/shard_map/dot_general | solution.py:32
  422.4 2.4 add_convert_fusion
  424.7 4.8 all-to-all-start.4
  431.5 77.8 %all-reduce.11 = (bf16[768]{0:T(1024)(128)(2,1)S(1)}, bf16[768]{0:T(1024)(128)(2,1)S(1)}, bf16[768]{0:T(1024)(128)(2,1)S(1)}, bf16[768]{0:T(1024)(128)(2,1)S(1)}...) all-reduce(bf16[768]{0:T(1024)(128)(2,1)S(1)} %dynamic-update-slice, ...), channel_id=1, replica_groups=mesh['replica'=4,'fsdp'=8] {'fsdp'}, use_global_device_ids=true, to_apply=%add.4 | all-reduce | flops 7680 | bytes 30720
  509.3 10.0 %add_convert_fusion.1 = bf16[1024,768]{1,0:T(8,128)(2,1)} fusion(f32[1024,768]{1,0:T(8,128)} %copy-done.9, bf16[1024,3072]{1,0:T(8,128)(2,1)} %get-tuple-element.59, bf16[6144,768]{1,0:T(8,128)(2,1)} %constant_dynamic-update-slice_fusion, s32[]{:T(128)S(6)} %select_n.106, f32[768]{0:T(1024)S(1)} %convert_element_type.196), kind=kOutput, calls=%fused_computation.56 | convolution fusion | flops 4834197504 | bytes 15731716 | tf_op jit(solution)/shard_map/dot_general | solution.py:198
  519.4 4.4 all-to-all-start.2
  523.9 28.6 %reduce-scatter.5.cloned.1.call-done = bf16[96,2304]{1,0:T(8,128)(2,1)} async-done(((bf16[768,2304]{1,0:T(8,128)(2,1)}), bf16[96,2304]{1,0:T(8,128)(2,1)}) %reduce-scatter.5.cloned.1.call-update) | async-done | bytes 442384 | tf_op jit(solution)/shard_map/reduce_scatter | solution.py:289
  552.6 102.3 %reduce-scatter.9.cloned.1.call-done = bf16[96,3072]{1,0:T(8,128)(2,1)} async-done(((bf16[768,3072]{1,0:T(8,128)(2,1)}), bf16[96,3072]{1,0:T(8,128)(2,1)}) %reduce-scatter.9.cloned.1.call-update) | async-done | bytes 589840 | tf_op jit(solution)/shard_map/reduce_scatter | solution.py:301
  654.9 98.8 %reduce-scatter.11.cloned.1.call-done = bf16[384,768]{1,0:T(8,128)(2,1)} async-done(((bf16[3072,768]{1,0:T(8,128)(2,1)}), bf16[384,768]{1,0:T(8,128)(2,1)}) %reduce-scatter.11.cloned.1.call-update) | async-done | bytes 589840 | tf_op jit(solution)/shard_map/reduce_scatter | solution.py:307
  756.7 6.5 all-reduce.13
  773.4 29.4 %all-reduce.17.cloned.1.call-done = (bf16[96,2304]{1,0:T(8,128)(2,1)}, bf16[96,768]{1,0:T(8,128)(2,1)}, bf16[96,3072]{1,0:T(8,128)(2,1)}, bf16[384,768]{1,0:T(8,128)(2,1)}) async-done(((bf16[96,2304]{1,0:T(8,128)(2,1)}, bf16[96,768]{1,0:T(8,128)(2,1)}, bf16[96,3072]{1,0:T(8,128)(2,1)}, bf16[384,768]{1,0:T(8,128)(2,1)}), (bf16[96,2304]{1,0:T(8,128)(2,1)}, bf16[96,768]{1,0:T(8,128)(2,1)}, ...) | async-done | bytes 1769488 | tf_op jit(solution)/shard_map/psum | solution.py:317
  806.5 2.2 convert_element_type.218
  (236 shorter events, 92.3 us)
Async XLA Ops:
  7.2 58.5 %copy-start = (bf16[1024,768]{1,0:T(8,128)(2,1)S(1)}, bf16[1024,768]{1,0:T(8,128)(2,1)}, u32[]{:S(2)}) copy-start(bf16[1024,768]{1,0:T(8,128)(2,1)} %param.16) | copy-start | bytes 4718596
  7.2 222.2 %all-gather.5.cloned.1.call-start = ((), (), s32[]{:S(2)}) async-start(), calls=%async_computation.9 | async-start | bytes 3981312 | tf_op jit(solution)/shard_map/all_gather | solution.py:142
  7.9 248.8 %all-gather.7.cloned.1.call-start = ((), (), s32[]{:S(2)}) async-start(), calls=%async_computation.10 | async-start | bytes 1327104 | tf_op jit(solution)/shard_map/all_gather | solution.py:143
  8.7 33.3 %collective-permute-start = (bf16[384,768]{1,0:T(8,128)(2,1)}, bf16[384,768]{1,0:T(8,128)(2,1)S(1)}, u32[]{:S(2)}, u32[]{:S(2)}) collective-permute-start(bf16[384,768]{1,0:T(8,128)(2,1)} %param.30), channel_id=1, source_target_pairs={{0,1},{1,2},{2,3},{3,4},{4,5},{5,6},{6,7},{7,0},{8,9},{9,10},{10,1... | collective-permute-start | bytes 1769480 | tf_op jit(solution)/shard_map/ppermute | solution.py:18
  11.7 63.6 %collective-permute-start.4 = (bf16[384,768]{1,0:T(8,128)(2,1)}, bf16[384,768]{1,0:T(8,128)(2,1)}, u32[]{:S(2)}, u32[]{:S(2)}) collective-permute-start(bf16[384,768]{1,0:T(8,128)(2,1)} %param.30), channel_id=1, source_target_pairs={{0,7},{1,0},{2,1},{3,2},{4,3},{5,4},{6,5},{7,6},{8,15},{9,8},{10,9... | collective-permute-start | bytes 1769480 | tf_op jit(solution)/shard_map/ppermute | solution.py:20
  16.6 27.8 %copy-start.35 = (s32[128]{0:T(128)}, s32[128]{0:T(128)S(1)}, u32[]{:S(2)}) copy-start(s32[128]{0:T(128)S(1)} %fusion.54) | copy-start | bytes 1540
  42.0 25.6 %copy-start.20 = (bf16[384,768]{1,0:T(8,128)(2,1)}, bf16[384,768]{1,0:T(8,128)(2,1)S(1)}, u32[]{:S(2)}) copy-start(bf16[384,768]{1,0:T(8,128)(2,1)S(1)} %collective-permute-done) | copy-start | bytes 1769476
  42.0 23.5 %collective-permute-start.1 = (bf16[384,768]{1,0:T(8,128)(2,1)S(1)}, bf16[384,768]{1,0:T(8,128)(2,1)}, u32[]{:S(2)}, u32[]{:S(2)}) collective-permute-start(bf16[384,768]{1,0:T(8,128)(2,1)S(1)} %collective-permute-done), channel_id=1, source_target_pairs={{0,1},{1,2},{2,3},{3,4},{4,5},{5,6},{6,7},{7,0},{8,9},{9,10},{10,1... | collective-permute-start | bytes 1769480 | tf_op jit(solution)/shard_map/ppermute | solution.py:18
  46.3 21.2 %all-to-all-start.1 = ((s32[8,16,1]{1,2,0:T(1,128)}), s32[8,16,1]{1,2,0:T(1,128)S(1)}, u32[]{:S(2)}, u32[]{:S(2)}) async-start(s32[8,16,1]{1,2,0:T(1,128)} %bitcast.11), calls=%async_computation.1 | async-start | bytes 8192 | tf_op jit(solution)/shard_map/all_to_all | solution.py:126
  51.2 238.6 %all-gather.9.cloned.1.call-start = ((), (), s32[]{:S(2)}) async-start(), calls=%async_computation.11 | async-start | bytes 5308416 | tf_op jit(solution)/shard_map/all_gather | solution.py:146
  65.5 43.3 %collective-permute-start.2 = (bf16[384,768]{1,0:T(8,128)(2,1)}, bf16[384,768]{1,0:T(8,128)(2,1)}, u32[]{:S(2)}, u32[]{:S(2)}) collective-permute-start(bf16[384,768]{1,0:T(8,128)(2,1)} %collective-permute-done.1), channel_id=1, source_target_pairs={{0,1},{1,2},{2,3},{3,4},{4,5},{5,6},{6,7},{7,0},{8,9},{9,10},{10,1... | collective-permute-start | bytes 1769480 | tf_op jit(solution)/shard_map/ppermute | solution.py:18
  65.7 8.0 copy-start.31
  67.5 44.1 %copy-start.34 = (bf16[384]{0:T(512)(128)(2,1)S(1)}, bf16[384]{0:T(512)(128)(2,1)}, u32[]{:S(2)}) copy-start(bf16[384]{0:T(512)(128)(2,1)} %param.29) | copy-start | bytes 2308
  67.5 44.1 %copy-start.33 = (u32[32]{0:T(128)S(1)}, u32[32]{0:T(128)}, u32[]{:S(2)}) copy-start(u32[32]{0:T(128)} %constant.191) | copy-start | bytes 388
  67.5 45.4 %copy-start.40 = (bf16[96]{0:T(256)(128)(2,1)S(1)}, bf16[96]{0:T(256)(128)(2,1)}, u32[]{:S(2)}) copy-start(bf16[96]{0:T(256)(128)(2,1)} %param.26) | copy-start | bytes 580
  67.5 45.6 %copy-start.41 = (bf16[96]{0:T(256)(128)(2,1)S(1)}, bf16[96]{0:T(256)(128)(2,1)}, u32[]{:S(2)}) copy-start(bf16[96]{0:T(256)(128)(2,1)} %param.27) | copy-start | bytes 580
  67.5 45.8 %copy-start.42 = (bf16[96]{0:T(256)(128)(2,1)S(1)}, bf16[96]{0:T(256)(128)(2,1)}, u32[]{:S(2)}) copy-start(bf16[96]{0:T(256)(128)(2,1)} %param.22) | copy-start | bytes 580
  67.5 46.1 %copy-start.43 = (bf16[96]{0:T(256)(128)(2,1)S(1)}, bf16[96]{0:T(256)(128)(2,1)}, u32[]{:S(2)}) copy-start(bf16[96]{0:T(256)(128)(2,1)} %param.23) | copy-start | bytes 580
  67.6 148.3 %all-to-all-start = ((bf16[8,128,768]{2,1,0:T(8,128)(2,1)}), bf16[8,128,768]{2,1,0:T(8,128)(2,1)S(1)}, u32[]{:S(2)}, u32[]{:S(2)}) async-start(bf16[8,128,768]{2,1,0:T(8,128)(2,1)} %bitcast.8), calls=%async_computation | async-start | bytes 3145728 | tf_op jit(solution)/shard_map/all_to_all | solution.py:125
  75.4 111.5 %collective-permute-start.5 = (bf16[384,768]{1,0:T(8,128)(2,1)}, bf16[384,768]{1,0:T(8,128)(2,1)}, u32[]{:S(2)}, u32[]{:S(2)}) collective-permute-start(bf16[384,768]{1,0:T(8,128)(2,1)} %collective-permute-done.4), channel_id=1, source_target_pairs={{0,7},{1,0},{2,1},{3,2},{4,3},{5,4},{6,5},{7,6},{8,15},{9,8},{10,9... | collective-permute-start | bytes 1769480 | tf_op jit(solution)/shard_map/ppermute | solution.py:20
  108.8 81.4 %collective-permute-start.3 = (bf16[384,768]{1,0:T(8,128)(2,1)}, bf16[384,768]{1,0:T(8,128)(2,1)}, u32[]{:S(2)}, u32[]{:S(2)}) collective-permute-start(bf16[384,768]{1,0:T(8,128)(2,1)} %collective-permute-done.2), channel_id=1, source_target_pairs={{0,1},{1,2},{2,3},{3,4},{4,5},{5,6},{6,7},{7,0},{8,9},{9,10},{10,1... | collective-permute-start | bytes 1769480 | tf_op jit(solution)/shard_map/ppermute | solution.py:18
  151.5 74.3 %copy-start.27 = (f32[768]{0:T(1024)}, f32[768]{0:T(1024)S(1)}, u32[]{:S(2)}) copy-start(f32[768]{0:T(1024)S(1)} %convert_element_type.183) | copy-start | bytes 9220
  182.9 4.0 copy-start.37
  185.0 40.8 %copy-start.6 = (bf16[128,8,768]{2,1,0:T(8,128)(2,1)}, bf16[128,8,768]{2,1,0:T(8,128)(2,1)S(1)}, u32[]{:S(2)}) copy-start(bf16[128,8,768]{2,1,0:T(8,128)(2,1)S(1)} %gather_fusion.2) | copy-start | bytes 4718596
  185.0 11.0 %copy-start.21 = (bf16[384,768]{1,0:T(8,128)(2,1)S(1)}, bf16[384,768]{1,0:T(8,128)(2,1)}, u32[]{:S(2)}) copy-start(bf16[384,768]{1,0:T(8,128)(2,1)} %copy-done.20) | copy-start | bytes 1769476
  186.9 10.0 %copy-start.19 = (bf16[384,768]{1,0:T(8,128)(2,1)S(1)}, bf16[384,768]{1,0:T(8,128)(2,1)}, u32[]{:S(2)}) copy-start(bf16[384,768]{1,0:T(8,128)(2,1)} %param.30) | copy-start | bytes 1769476
  186.9 15.7 %collective-permute-start.6 = (bf16[384,768]{1,0:T(8,128)(2,1)}, bf16[384,768]{1,0:T(8,128)(2,1)S(1)}, u32[]{:S(2)}, u32[]{:S(2)}) collective-permute-start(bf16[384,768]{1,0:T(8,128)(2,1)} %collective-permute-done.5), channel_id=1, source_target_pairs={{0,7},{1,0},{2,1},{3,2},{4,3},{5,4},{6,5},{7,6},{8,15},{9,8},{10,9... | collective-permute-start | bytes 1769480 | tf_op jit(solution)/shard_map/ppermute | solution.py:20
  215.8 10.0 %copy-start.3 = (bf16[8,128,768]{2,1,0:T(8,128)(2,1)}, bf16[8,128,768]{2,1,0:T(8,128)(2,1)S(1)}, u32[]{:S(2)}) copy-start(bf16[8,128,768]{2,1,0:T(8,128)(2,1)S(1)} %all-to-all-done) | copy-start | bytes 4718596
  215.8 111.3 %all-to-all-start.3 = ((bf16[8,128,768]{2,1,0:T(8,128)(2,1)}), bf16[8,128,768]{2,1,0:T(8,128)(2,1)}, u32[]{:S(2)}, u32[]{:S(2)}) async-start(bf16[8,128,768]{2,1,0:T(8,128)(2,1)} %bitcast.183), calls=%async_computation.3 | async-start | bytes 3145728 | tf_op jit(solution)/shard_map/all_to_all | solution.py:206
  222.2 301.7 %reduce-scatter.7.cloned.1.call-start = ((), (), s32[]{:S(2)}) async-start(), calls=%async_computation.13 | async-start | bytes 1327104 | tf_op jit(solution)/shard_map/reduce_scatter | solution.py:292
  327.1 13.0 %copy-start.10 = (f32[1024,768]{1,0:T(8,128)S(1)}, f32[1024,768]{1,0:T(8,128)}, u32[]{:S(2)}) copy-start(f32[1024,768]{1,0:T(8,128)} %copy-done.9) | copy-start | bytes 9437188
  327.1 13.0 %copy-start.38 = (bf16[768,3072]{1,0:T(8,128)(2,1)S(1)}, bf16[768,3072]{1,0:T(8,128)(2,1)}, u32[]{:S(2)}) copy-start(bf16[768,3072]{1,0:T(8,128)(2,1)} %all-gather.9.cloned.1.call-done) | copy-start | bytes 14155780
  340.1 5.7 copy-start.45
  356.8 5.2 copy-start.18
  369.2 183.4 %reduce-scatter.5.cloned.1.call-start = ((), (), s32[]{:S(2)}) async-start(), calls=%async_computation.12 | async-start | bytes 3981312 | tf_op jit(solution)/shard_map/reduce_scatter | solution.py:289
  370.9 6.5 copy-start.14
  392.1 262.8 %reduce-scatter.9.cloned.1.call-start = ((), (), s32[]{:S(2)}) async-start(), calls=%async_computation.14 | async-start | bytes 5308416 | tf_op jit(solution)/shard_map/reduce_scatter | solution.py:301
  402.9 350.9 %reduce-scatter.11.cloned.1.call-start = ((), (), s32[]{:S(2)}) async-start(), calls=%async_computation.15 | async-start | bytes 5308416 | tf_op jit(solution)/shard_map/reduce_scatter | solution.py:307
  414.0 8.4 %copy-start.12 = (f32[1024,768]{1,0:T(8,128)S(1)}, f32[1024,768]{1,0:T(8,128)}, u32[]{:S(2)}) copy-start(f32[1024,768]{1,0:T(8,128)} %copy-done.11) | copy-start | bytes 9437188
  424.7 4.9 copy-start.44
  424.7 94.7 %all-to-all-start.4 = ((bf16[8,128,768]{2,1,0:T(8,128)(2,1)}), bf16[8,128,768]{2,1,0:T(8,128)(2,1)S(1)}, u32[]{:S(2)}, u32[]{:S(2)}) async-start(bf16[8,128,768]{2,1,0:T(8,128)(2,1)} %bitcast.172), calls=%async_computation.4 | async-start | bytes 3145728 | tf_op jit(solution)/shard_map/all_to_all | solution.py:280
  519.4 235.7 %copy-start.36 = (s32[128]{0:T(128)S(1)}, s32[128]{0:T(128)}, u32[]{:S(2)}) copy-start(s32[128]{0:T(128)} %copy-done.35) | copy-start | bytes 1540
  519.4 246.9 %copy-start.8 = (bf16[1024,768]{1,0:T(8,128)(2,1)S(1)}, bf16[1024,768]{1,0:T(8,128)(2,1)}, u32[]{:S(2)}) copy-start(bf16[1024,768]{1,0:T(8,128)(2,1)} %add_convert_fusion) | copy-start | bytes 4718596
  519.4 250.5 %all-to-all-start.2 = ((bf16[8,128,768]{2,1,0:T(8,128)(2,1)}), bf16[8,128,768]{2,1,0:T(8,128)(2,1)}, u32[]{:S(2)}, u32[]{:S(2)}) async-start(bf16[8,128,768]{2,1,0:T(8,128)(2,1)} %bitcast.191), calls=%async_computation.2 | async-start | bytes 3145728 | tf_op jit(solution)/shard_map/all_to_all | solution.py:201
  523.9 278.9 %all-reduce.17.cloned.1.call-start = ((), (), s32[]{:S(2)}) async-start(), calls=%async_computation.16 | async-start | bytes 3538944 | tf_op jit(solution)/shard_map/psum | solution.py:317
  768.1 3.9 copy-start.32
  772.0 37.7 %copy-start.1 = (bf16[1024,768]{1,0:T(8,128)(2,1)S(1)}, bf16[1024,768]{1,0:T(8,128)(2,1)}, u32[]{:S(2)}) copy-start(bf16[1024,768]{1,0:T(8,128)(2,1)} %param.16) | copy-start | bytes 4718596
  802.8 5.9 copy-start.23
  (18 other events, 34.9 us)
Sparse Core Ops, SparseCore 0:
  10.2 115.4 all-gather.4
  127.9 56.7 all-gather.6
  186.9 102.8 all-gather.8
  369.3 64.1 reduce-scatter.6
  437.0 115.5 reduce-scatter.4
  556.1 98.7 reduce-scatter.8
  658.6 95.1 reduce-scatter.10
  756.4 46.3 all-reduce.16
